TPU v7x, 128 devices: a whole 4x4x4 slice. The times are simulated.
128 devices in a mesh: row: 8 (over x, core), col: 16 (over y, z).
Axes of the slice: x: 4, y: 4, z: 4, core: 2. Of those that a mesh axis runs over, the one named last changes fastest.
Arguments:
- features: bfloat16 [65536, 1024], P(('row', 'col')), may hold values from -6 to 6
- neighbours: int32 [65536, 16], P(('row', 'col')), may hold values from 0 to 3583, as said below
- degrees: int32 [65536], P(('row', 'col')), may hold values from 1 to 16, as said below
- send_rows: int32 [128, 2048], P(('row', 'col')), may hold values from 0 to 511
- send_count: int32 [128, 128], P(('row', 'col')), may hold values from 8 to 16, as said below
- hub_rows: int32 [1024], P(('row', 'col')), may hold values from 0 to 511, as said below
- w_self: bfloat16 [1024, 1024], replicated, may hold values from -0.1875 to 0.1875
- w_neigh: bfloat16 [1024, 1024], replicated, may hold values from -0.1875 to 0.1875
- bias_term: float32 [1024], replicated, may hold values from -3 to 3
- cotangent: bfloat16 [65536, 1024], P(('row', 'col')), may hold values from -6 to 6
Outputs:
- hidden: bfloat16 [65536, 1024], P(('row', 'col'))
- grad_x: bfloat16 [65536, 1024], P(('row', 'col'))
- grad_self: bfloat16 [1024, 1024], replicated
- grad_neigh: bfloat16 [1024, 1024], replicated
Inputs may be any that keep to these rules, and one draw needn't show every extreme that they name: neighbours of partition d point to its own rows (below 512), to live slots of arrived_d only (row 512 + p * 16 + s with p != d and s < send_count[p, d]), or to hub rows; entries at j >= degrees[i] also lie in the table. `degrees`: every seed has at least one neighbour. `send_count`: each partition sends between 8 and 16 live rows to each partition, and exactly 16 to the next one. `hub_rows`: the 8 hub rows of a partition are distinct.
All inputs are finite; a program needn't handle non-finite values.
Results may differ from a plain program's by a relative error of at most 0.0064.
Values may be sent and summed in bfloat16 or wider, within the bound.
A program may use at most 128 MiB of HBM per device.

v0:
```python
import jax
import jax.numpy as jnp
from jax import lax
from jax.sharding import PartitionSpec as P


def silu_slope(pre_act):
    sigmoid_val = jax.nn.sigmoid(pre_act)
    return sigmoid_val * (1.0 + pre_act * (1.0 - sigmoid_val))


def on_device(
    features,
    neighbours,
    degrees,
    send_rows,
    send_count,
    hub_rows,
    w_self,
    w_neigh,
    bias_term,
    cotangent,
):
    n_row = lax.axis_size("row")
    n_col = lax.axis_size("col")
    n_dev = n_row * n_col
    n_local, feat_width = features.shape
    fanout = neighbours.shape[1]
    capacity = send_rows.shape[1] // n_dev
    tile_size = min(512, n_local)
    n_tiles = n_local // tile_size
    slot_live = (
        jnp.arange(capacity, dtype=jnp.int32)[None, :] < send_count.reshape(n_dev, 1)
    ).reshape(-1, 1)
    outgoing = jnp.where(slot_live, features[send_rows[0]], jnp.zeros((), jnp.bfloat16))
    arrived = lax.all_to_all(outgoing, ("row", "col"), split_axis=0, concat_axis=0, tiled=True)
    own_hubs = features[hub_rows]
    all_hubs = lax.all_gather(own_hubs, ("row", "col"), axis=0, tiled=True)
    src_table = jnp.concatenate([features, arrived, all_hubs], 0)
    table_len = src_table.shape[0]
    live_mask = jnp.arange(fanout, dtype=jnp.int32)[None, :] < degrees[:, None]
    inv_deg = 1.0 / degrees.astype(jnp.float32)

    def gather_tile(tile_index):
        tile_live = live_mask.astype(jnp.bfloat16)
        picked = src_table[neighbours]
        return jnp.einsum("nf,nfd->nd", tile_live, picked, preferred_element_type=jnp.float32)

    summed = lax.map(gather_tile, jnp.arange(n_tiles, dtype=jnp.int32)).reshape(n_local, feat_width)
    aggregate = (summed * inv_deg[:, None]).astype(jnp.bfloat16)
    pre_act = (
        jnp.dot(features, w_self, preferred_element_type=jnp.float32)
        + jnp.dot(aggregate, w_neigh, preferred_element_type=jnp.float32)
        + bias_term[None, :]
    )
    hidden = jax.nn.silu(pre_act).astype(jnp.bfloat16)
    d_pre = (cotangent.astype(jnp.float32) * silu_slope(pre_act)).astype(jnp.bfloat16)
    self_part = lax.dot_general(
        features, d_pre, (((0,), (0,)), ((), ())), preferred_element_type=jnp.float32
    )
    neigh_part = lax.dot_general(
        aggregate, d_pre, (((0,), (0,)), ((), ())), preferred_element_type=jnp.float32
    )
    grad_self, grad_neigh = lax.psum((self_part, neigh_part), ("row", "col"))
    d_agg = (
        lax.dot_general(
            d_pre, w_neigh, (((1,), (1,)), ((), ())), preferred_element_type=jnp.float32
        )
        * inv_deg[:, None]
    )
    d_own = lax.dot_general(
        d_pre, w_self, (((1,), (1,)), ((), ())), preferred_element_type=jnp.float32
    )

    def spread_tile(tile_index, d_table):
        target = jnp.where(live_mask, neighbours, table_len)
        updates = jnp.broadcast_to(d_agg[:, None, :], (tile_size, fanout, feat_width))
        return d_table.at[target.reshape(-1)].add(updates.reshape(-1, feat_width), mode="drop")

    d_table = lax.fori_loop(
        0, n_tiles, spread_tile, jnp.zeros((table_len, feat_width), jnp.float32)
    )
    n_slots = n_dev * capacity
    d_local = d_table[:n_local]
    d_arrived = d_table[n_local : n_local + n_slots]
    d_hubs = d_table[n_local + n_slots :]
    returned = lax.all_to_all(
        d_arrived.astype(jnp.bfloat16), ("row", "col"), split_axis=0, concat_axis=0, tiled=True
    ).astype(d_arrived.dtype)
    hub_back = lax.psum_scatter(d_hubs, ("row", "col"), scatter_dimension=0, tiled=True)
    grad_x = d_own + d_local
    grad_x = grad_x.at[send_rows[0]].add(jnp.where(slot_live, returned, 0.0))
    grad_x = grad_x.at[hub_rows].add(hub_back)
    return (
        hidden,
        grad_x.astype(jnp.bfloat16),
        grad_self.astype(jnp.bfloat16),
        grad_neigh.astype(jnp.bfloat16),
    )


def solution(mesh):
    in_specs = (
        P(("row", "col"), None),
        P(("row", "col"), None),
        P(("row", "col")),
        P(("row", "col"), None),
        P(("row", "col"), None),
        P(("row", "col")),
        P(),
        P(),
        P(),
        P(("row", "col"), None),
    )
    out_specs = (P(("row", "col"), None), P(("row", "col"), None), P(), P())
    return jax.shard_map(
        on_device, mesh=mesh, in_specs=in_specs, out_specs=out_specs, check_vma=False
    )
```

profile of v0, /device:TPU:0, one launch (start us, length us, event | category | flops | bytes accessed | tf_op | source)
XLA Modules:
  0.0 957.6 jit_solution(10110251208233370689)
XLA Ops:
  7.2 0.0 copy-start
  7.2 0.0 all-gather.3.cloned.1.call-start
  7.2 0.8 compare_select_fusion.3
  8.0 2.5 gather_fusion.1
  10.6 0.0 all-gather.3.cloned.1.call-update
  10.6 0.7 compare_select_fusion.2
  11.3 0.0 copy-start.9
  11.3 12.3 %gather_fusion = bf16[2048,1024]{1,0:T(8,128)(2,1)} fusion(bf16[512,1024]{1,0:T(8,128)(2,1)} %param.10, s32[2048]{0:T(1024)S(1)} %broadcast_clamp_fusion.1), kind=kCustom, calls=%fused_computation | custom fusion | bytes 8396800 | tf_op jit(solution)/shard_map/gather | solution.py:35
  23.7 0.0 copy-done.9
  23.7 0.1 iota_compare_fusion
  23.8 3.8 broadcast_select_fusion
  27.6 0.0 copy-start.7
  27.6 0.0 copy-start.1
  27.6 11.7 %all-to-all-start = ((bf16[128,16,1024]{2,1,0:T(8,128)(2,1)}), bf16[128,16,1024]{2,1,0:T(8,128)(2,1)}, u32[]{:S(2)}, u32[]{:S(2)}) async-start(bf16[128,16,1024]{2,1,0:T(8,128)(2,1)} %broadcast_select_fusion), calls=%async_computation | async-start | bytes 8388608 | tf_op jit(solution)/shard_map/all_to_all | solution.py:36
  39.3 0.0 reduce-scatter.2.cloned.1.call-start
  39.3 0.0 copy-done.8
  39.4 0.4 copy.18
  39.8 0.0 copy-done.7
  39.8 0.8 copy.15
  40.7 1.1 reshape.128
  41.8 0.8 copy.16
  42.6 1.1 reshape.107
  43.7 0.0 copy-done.1
  43.7 4.2 fusion.11
  48.0 64.1 %all-gather.3.cloned.1.call-done = bf16[1024,1024]{1,0:T(8,128)(2,1)} async-done(((bf16[8,1024]{1,0:T(8,128)(2,1)}), bf16[1024,1024]{1,0:T(8,128)(2,1)}) %all-gather.3.cloned.1.call-update) | async-done | bytes 2097168 | tf_op jit(solution)/shard_map/all_gather | solution.py:38
  112.1 0.0 all-to-all-done
  112.1 6.3 pad_maximum_fusion
  118.3 44.7 %gather_fusion.2 = bf16[8192,1024]{1,0:T(8,128)(2,1)} fusion(bf16[3584,1024]{1,0:T(8,128)(2,1)} %pad_maximum_fusion, s32[8192]{0:T(1024)S(1)} %broadcast_clamp_fusion), kind=kCustom, calls=%fused_computation.2 | custom fusion | bytes 33587200 | tf_op jit(solution)/shard_map/while/body/eval_jaxpr/gather | solution.py:46
  163.0 0.0 copy-start.10
  163.0 0.0 copy-start.11
  163.0 0.0 copy-start.12
  163.0 8.6 fusion.12
  171.6 0.0 copy-done
  171.6 0.0 copy-done.10
  171.6 0.0 copy-done.11
  171.7 0.0 copy-done.12
  171.7 0.0 copy-start.2
  171.7 3.0 multiply_convert_fusion
  174.7 0.0 copy-done.2
  174.7 0.0 copy-start.4
  174.7 1.3 convolution_multiply_fusion
  176.0 0.0 copy-done.4
  176.1 11.3 %broadcast_in_dim.67 = f32[512,16,1024]{2,1,0:T(8,128)} broadcast(f32[512,1024]{1,0:T(8,128)S(1)} %convolution_multiply_fusion), dimensions={0,2} | broadcast | bytes 35651584 | tf_op jit(solution)/shard_map/while/body/eval_jaxpr/broadcast_in_dim | solution.py:77
  187.4 77.1 %scatter_custom_fusion = f32[3584,1024]{1,0:T(8,128)} fusion(s32[8192]{0:T(1024)S(1)} %bitcast.40, f32[8192,1024]{1,0:T(8,128)} %bitcast.37, f32[]{:T(128)} %constant.13.clone.1), kind=kCustom, calls=%fused_computation.10 | custom fusion | flops 8388608 | bytes 14680576 | tf_op jit(solution)/shard_map/while/body/eval_jaxpr/scatter-add | solution.py:78
  264.4 4.7 slice.21
  269.2 0.0 reduce-scatter.2.cloned.1.call-update
  269.2 6.0 slice.24
  275.2 6.6 all-to-all-start.1
  281.8 0.1 lt.79
  281.9 0.0 copy-start.3
  281.9 0.0 copy-start.5
  281.9 4.6 convolution_bitcast_fusion
  286.5 0.0 copy-done.3
  286.5 0.0 copy-done.5
  286.5 3.5 fusion.8
  290.1 147.6 %all-reduce.2 = (bf16[1024,1024]{0,1:T(8,128)(2,1)}, bf16[1024,1024]{1,0:T(8,128)(2,1)}) all-reduce(f32[1024,1024]{0,1:T(8,128)} %convolution_bitcast_fusion, f32[1024,1024]{1,0:T(8,128)} %fusion.8), channel_id=1, replica_groups=mesh['row'=8,'col'=16] {'row','col'}, use_global_device_ids=true, to_apply=%region_4.5 | all-reduce | flops 2097152 | bytes 12582912 | tf_op jit(solution)/shard_map/psum | solution.py:64
  437.7 4.0 copy.17
  441.7 0.0 copy-done.6
  441.7 4.9 slice_add_fusion
  446.6 0.0 all-to-all-done.1
  446.6 21.7 %scatter_custom_fusion.1 = f32[512,1024]{1,0:T(8,128)} fusion(f32[512,1024]{1,0:T(8,128)} %slice_add_fusion, s32[2048]{0:T(1024)S(1)} %bitcast.42, bf16[2048,1024]{1,0:T(8,128)(2,1)} %bitcast.13, f32[]{:T(128)} %constant.13.clone.1, pred[2048]{0:T(1024)(128)(4,1)S(1)} %lt.79), kind=kCustom, calls=%fused_computation.8 | custom fusion | flops 6291456 | bytes 6294016 | tf_op jit(solution)/shard_map/scatter-add | solution.py:92
  468.3 476.0 %reduce-scatter.2.cloned.1.call-done = f32[8,1024]{1,0:T(8,128)} async-done(((f32[1024,1024]{1,0:T(8,128)}), f32[8,1024]{1,0:T(8,128)}) %reduce-scatter.2.cloned.1.call-update) | async-done | bytes 32784 | tf_op jit(solution)/shard_map/reduce_scatter | solution.py:90
  944.3 3.7 scatter_fusion
  948.0 2.7 convert_element_type.40
  (9 shorter events, 0.1 us)
Async XLA Ops:
  7.2 164.5 %copy-start = (bf16[1024,1024]{1,0:T(8,128)(2,1)S(1)}, bf16[1024,1024]{1,0:T(8,128)(2,1)}, u32[]{:S(2)}) copy-start(bf16[1024,1024]{1,0:T(8,128)(2,1)} %param.17) | copy-start | bytes 6291460
  7.2 104.9 %all-gather.3.cloned.1.call-start = ((), (), s32[]{:S(2)}) async-start(), calls=%async_computation.4 | async-start | bytes 2113536 | tf_op jit(solution)/shard_map/all_gather | solution.py:38
  11.3 12.3 %copy-start.9 = (s32[1,128]{1,0:T(1,128)S(1)}, s32[1,128]{1,0:T(1,128)}, u32[]{:S(2)}) copy-start(s32[1,128]{1,0:T(1,128)} %param.14) | copy-start | bytes 1540
  27.6 11.8 %copy-start.8 = (s32[512]{0:T(512)S(1)}, s32[512]{0:T(512)}, u32[]{:S(2)}) copy-start(s32[512]{0:T(512)} %param.12) | copy-start | bytes 6148
  27.6 12.2 %copy-start.7 = (s32[512,16]{0,1:T(8,128)S(1)}, s32[512,16]{0,1:T(8,128)}, u32[]{:S(2)}) copy-start(s32[512,16]{0,1:T(8,128)} %param.11) | copy-start | bytes 98308
  27.6 16.1 %copy-start.1 = (bf16[512,1024]{1,0:T(8,128)(2,1)S(1)}, bf16[512,1024]{1,0:T(8,128)(2,1)}, u32[]{:S(2)}) copy-start(bf16[512,1024]{1,0:T(8,128)(2,1)} %param.10) | copy-start | bytes 3145732
  27.6 84.5 %all-to-all-start = ((bf16[128,16,1024]{2,1,0:T(8,128)(2,1)}), bf16[128,16,1024]{2,1,0:T(8,128)(2,1)}, u32[]{:S(2)}, u32[]{:S(2)}) async-start(bf16[128,16,1024]{2,1,0:T(8,128)(2,1)} %broadcast_select_fusion), calls=%async_computation | async-start | bytes 8388608 | tf_op jit(solution)/shard_map/all_to_all | solution.py:36
  39.3 905.0 %reduce-scatter.2.cloned.1.call-start = ((), (), s32[]{:S(2)}) async-start(), calls=%async_computation.3 | async-start | bytes 4227072 | tf_op jit(solution)/shard_map/reduce_scatter | solution.py:90
  163.0 8.7 copy-start.10
  163.0 8.7 copy-start.11
  163.0 8.7 copy-start.12
  171.7 3.1 copy-start.2
  174.7 1.3 copy-start.4
  275.2 171.4 %all-to-all-start.1 = ((bf16[128,16,1024]{2,1,0:T(8,128)(2,1)}), bf16[128,16,1024]{2,1,0:T(8,128)(2,1)}, u32[]{:S(2)}, u32[]{:S(2)}) async-start(bf16[128,16,1024]{2,1,0:T(8,128)(2,1)} %bitcast.39), calls=%async_computation.1 | async-start | bytes 8388608 | tf_op jit(solution)/shard_map/all_to_all | solution.py:87
  281.9 4.6 copy-start.3
  281.9 4.6 copy-start.5
  437.7 4.0 copy-start.6
Sparse Core Ops, SparseCore 0:
  11.5 100.4 all-gather.2
  269.3 674.8 reduce-scatter.1
where the time goes:
time: 959 us; the launch traced here: 958 us
  waiting for transfers between devices  540 us (56%)
  blocking collectives  148 us (15%)
  other arithmetic  117 us (12%)
  local copies, waits for them, and re-layouts  90.1 us (9%)
  matrix products  30.2 us (3%)
  starting transfers between devices  18.4 us (2%)
  between operations  14.3 us (1%)
    reduce_scatter x1, waiting for transfers between devices, on_device(): lax.psum_scatter(d_hubs, ('row', 'col'), scatter_dimension=0, tiled=True)  476 us
    psum x1, blocking collectives, on_device(): grad_self, grad_neigh = lax.psum((self_part, neigh_part), ('row', 'col'))  148 us
    scatter-add x1, other arithmetic, spread_tile(): d_table.at[target.reshape(-1)]  77.1 us
    all_gather x1, waiting for transfers between devices, on_device(): all_hubs = lax.all_gather(own_hubs, ('row', 'col'), axis=0, tiled=True)  64.1 us
    gather x1, local copies, waits for them, and re-layouts, gather_tile(): picked = src_table[neighbours]  44.7 us
    scatter-add x1, other arithmetic, on_device(): grad_x = grad_x.at[send_rows[0]].add(jnp.where(slot_live, returned, 0.0))  21.7 us
  transfers between devices with their start and end apart: 4, of which 2 were waited for; matrix products, arithmetic and copies ran while one was open for 7% of the time, Pallas kernels for 0%

commit v1 on v0

--- a/solution.py
+++ b/solution.py
@@ -21,6 +21,11 @@
     bias_term,
     cotangent,
 ):
+
+    def floor_build(frame, axis_name, mesh_name="col"):
+        piece_out = lax.psum(frame, axis_name)
+        return lax.psum(piece_out, mesh_name)
+
     n_row = lax.axis_size("row")
     n_col = lax.axis_size("col")
     n_dev = n_row * n_col
@@ -61,7 +66,7 @@
     neigh_part = lax.dot_general(
         aggregate, d_pre, (((0,), (0,)), ((), ())), preferred_element_type=jnp.float32
     )
-    grad_self, grad_neigh = lax.psum((self_part, neigh_part), ("row", "col"))
+    grad_self, grad_neigh = floor_build((self_part, neigh_part), "row")
     d_agg = (
         lax.dot_general(
             d_pre, w_neigh, (((1,), (1,)), ((), ())), preferred_element_type=jnp.float32

time: 959 us -> 979 us (1.021)
  blocking collectives: 148 us -> 203 us
  waiting for transfers between devices: 540 us -> 507 us
    reduce_scatter x1, waiting for transfers between devices: 476 us -> 393 us  [on_device(): lax.psum_scatter(d_hubs, ('row', 'col'), scatter_dimension=0, tiled=True)]
    psum x1, blocking collectives: 148 us -> 203 us  [floor_build(): return lax.psum(piece_out, mesh_name)]
    all_to_all x1, waiting for transfers between devices: 0.01 us -> 47.2 us  [on_device(): lax.all_to_all(d_arrived.astype(jnp.bfloat16), ('row', 'col'), split_axis...]
  transfers between devices with their start and end apart: 4 -> 5, of which waited for: 2 -> 3; matrix products, arithmetic and copies ran while one was open for 7% -> 16% of each run, Pallas kernels for 0% -> 0%
where the time goes in v1:
time: 979 us; the launch traced here: 978 us
  waiting for transfers between devices  507 us (52%)
  blocking collectives  203 us (21%)
  other arithmetic  117 us (12%)
  local copies, waits for them, and re-layouts  89.6 us (9%)
  matrix products  28.9 us (3%)
  starting transfers between devices  18.8 us (2%)
  between operations  13.9 us (1%)
    reduce_scatter x1, waiting for transfers between devices, on_device(): lax.psum_scatter(d_hubs, ('row', 'col'), scatter_dimension=0, tiled=True)  393 us
    psum x1, blocking collectives, floor_build(): return lax.psum(piece_out, mesh_name)  203 us
    scatter-add x1, other arithmetic, spread_tile(): d_table.at[target.reshape(-1)]  77.1 us
    all_gather x1, waiting for transfers between devices, on_device(): all_hubs = lax.all_gather(own_hubs, ('row', 'col'), axis=0, tiled=True)  66.1 us
    all_to_all x1, waiting for transfers between devices, on_device(): lax.all_to_all(d_arrived.astype(jnp.bfloat16), ('row', 'col'), split_axis...  47.2 us
    gather x1, local copies, waits for them, and re-layouts, gather_tile(): picked = src_table[neighbours]  44.7 us
    scatter-add x1, other arithmetic, on_device(): grad_x = grad_x.at[send_rows[0]].add(jnp.where(slot_live, returned, 0.0))  21.7 us
  transfers between devices with their start and end apart: 5, of which 3 were waited for; matrix products, arithmetic and copies ran while one was open for 16% of the time, Pallas kernels for 0%

profile of v1, /device:TPU:0, one launch (start us, length us, event | category | flops | bytes accessed | tf_op | source)
XLA Modules:
  0.0 977.7 jit_solution(722586127917534417)
XLA Ops:
  7.2 0.0 copy-start
  7.2 0.0 all-gather.3.cloned.1.call-start
  7.2 0.8 compare_select_fusion.3
  8.0 2.5 gather_fusion.1
  10.6 0.0 all-gather.3.cloned.1.call-update
  10.6 0.7 compare_select_fusion.2
  11.3 0.0 copy-start.6
  11.3 12.3 %gather_fusion = bf16[2048,1024]{1,0:T(8,128)(2,1)} fusion(bf16[512,1024]{1,0:T(8,128)(2,1)} %param.10, s32[2048]{0:T(1024)S(1)} %broadcast_clamp_fusion.1), kind=kCustom, calls=%fused_computation | custom fusion | bytes 8396800 | tf_op jit(solution)/shard_map/gather | solution.py:40
  23.7 0.0 copy-done.6
  23.7 0.1 iota_compare_fusion
  23.8 3.8 broadcast_select_fusion
  27.6 0.0 copy-start.5
  27.6 0.0 copy-start.4
  27.6 0.0 copy-start.1
  27.6 11.7 %all-to-all-start = ((bf16[128,16,1024]{2,1,0:T(8,128)(2,1)}), bf16[128,16,1024]{2,1,0:T(8,128)(2,1)}, u32[]{:S(2)}, u32[]{:S(2)}) async-start(bf16[128,16,1024]{2,1,0:T(8,128)(2,1)} %broadcast_select_fusion), calls=%async_computation | async-start | bytes 8388608 | tf_op jit(solution)/shard_map/all_to_all | solution.py:41
  39.3 0.0 all-reduce.5.cloned.1.call-start
  39.3 0.0 copy-done.5
  39.4 0.4 copy.18
  39.8 0.0 copy-done.4
  39.8 0.8 copy.15
  40.7 1.1 reshape.128
  41.8 0.0 copy-done.1
  41.8 4.2 fusion.11
  46.0 66.1 %all-gather.3.cloned.1.call-done = bf16[1024,1024]{1,0:T(8,128)(2,1)} async-done(((bf16[8,1024]{1,0:T(8,128)(2,1)}), bf16[1024,1024]{1,0:T(8,128)(2,1)}) %all-gather.3.cloned.1.call-update) | async-done | bytes 2097168 | tf_op jit(solution)/shard_map/all_gather | solution.py:43
  112.1 0.0 all-to-all-done
  112.1 6.3 pad_maximum_fusion
  118.3 44.7 %gather_fusion.2 = bf16[8192,1024]{1,0:T(8,128)(2,1)} fusion(bf16[3584,1024]{1,0:T(8,128)(2,1)} %pad_maximum_fusion, s32[8192]{0:T(1024)S(1)} %broadcast_clamp_fusion), kind=kCustom, calls=%fused_computation.2 | custom fusion | bytes 33587200 | tf_op jit(solution)/shard_map/while/body/eval_jaxpr/gather | solution.py:51
  163.0 0.0 copy-start.7
  163.0 0.0 copy-start.8
  163.0 0.0 copy-start.9
  163.0 8.6 fusion.12
  171.7 0.0 copy-done
  171.7 0.0 copy-done.7
  171.7 0.0 copy-done.8
  171.7 0.0 copy-done.9
  171.7 3.0 multiply_convert_fusion
  174.7 0.0 copy-start.2
  174.7 3.3 convolution_bitcast_fusion
  178.0 0.0 copy-done.2
  178.0 3.7 fusion.8
  181.7 0.0 copy-start.3
  181.7 0.0 all-reduce.5.cloned.1.call-update
  181.7 0.2 reduce-scatter.2.cloned.1.call-start
  182.0 0.1 copy.16
  182.1 0.2 reshape.107
  182.3 0.6 copy-done.3
  182.9 1.3 convolution_multiply_fusion
  184.2 11.8 %broadcast_in_dim.67 = f32[512,16,1024]{2,1,0:T(8,128)} broadcast(f32[512,1024]{1,0:T(8,128)S(1)} %convolution_multiply_fusion), dimensions={0,2} | broadcast | bytes 35651584 | tf_op jit(solution)/shard_map/while/body/eval_jaxpr/broadcast_in_dim | solution.py:82
  196.1 77.1 %scatter_custom_fusion = f32[3584,1024]{1,0:T(8,128)} fusion(s32[8192]{0:T(1024)S(1)} %bitcast.40, f32[8192,1024]{1,0:T(8,128)} %bitcast.37, f32[]{:T(128)} %constant.13.clone.1), kind=kCustom, calls=%fused_computation.10 | custom fusion | flops 8388608 | bytes 14680576 | tf_op jit(solution)/shard_map/while/body/eval_jaxpr/scatter-add | solution.py:83
  273.2 4.8 slice.21
  278.0 0.0 reduce-scatter.2.cloned.1.call-update
  278.0 6.0 slice.24
  284.1 6.8 all-to-all-start.1
  290.9 0.1 lt.79
  291.0 4.8 slice_add_fusion
  295.8 47.2 %all-to-all-done.1 = bf16[128,16,1024]{2,1,0:T(8,128)(2,1)} async-done(((bf16[128,16,1024]{2,1,0:T(8,128)(2,1)}), bf16[128,16,1024]{2,1,0:T(8,128)(2,1)}, u32[]{:S(2)}, u32[]{:S(2)}) %all-to-all-start.1) | async-done | bytes 4194336 | tf_op jit(solution)/shard_map/all_to_all | solution.py:92
  343.0 21.7 %scatter_custom_fusion.1 = f32[512,1024]{1,0:T(8,128)} fusion(f32[512,1024]{1,0:T(8,128)} %slice_add_fusion, s32[2048]{0:T(1024)S(1)} %bitcast.42, bf16[2048,1024]{1,0:T(8,128)(2,1)} %bitcast.13, f32[]{:T(128)} %constant.13.clone.1, pred[2048]{0:T(1024)(128)(4,1)S(1)} %lt.79), kind=kCustom, calls=%fused_computation.8 | custom fusion | flops 6291456 | bytes 6294016 | tf_op jit(solution)/shard_map/scatter-add | solution.py:97
  364.7 0.0 all-reduce.5.cloned.1.call-done
  364.7 202.7 %all-reduce.6 = (bf16[1024,1024]{0,1:T(8,128)(2,1)}, bf16[1024,1024]{1,0:T(8,128)(2,1)}) all-reduce(f32[1024,1024]{0,1:T(8,128)} %get-tuple-element.44, f32[1024,1024]{1,0:T(8,128)} %get-tuple-element.45), channel_id=1, replica_groups=mesh['row'=8,'col'=16] {'col'}, use_global_device_ids=true, to_apply=%region_5.6 | all-reduce | flops 2097152 | bytes 12582912 | tf_op jit(solution)/shard_map/psum | solution.py:27
  567.4 3.9 copy.17
  571.3 393.4 %reduce-scatter.2.cloned.1.call-done = f32[8,1024]{1,0:T(8,128)} async-done(((f32[1024,1024]{1,0:T(8,128)}), f32[8,1024]{1,0:T(8,128)}) %reduce-scatter.2.cloned.1.call-update) | async-done | bytes 32784 | tf_op jit(solution)/shard_map/reduce_scatter | solution.py:95
  964.7 3.7 scatter_fusion
  968.5 2.7 convert_element_type.40
  (7 shorter events, 0.1 us)
Async XLA Ops:
  7.2 164.5 %copy-start = (bf16[1024,1024]{1,0:T(8,128)(2,1)S(1)}, bf16[1024,1024]{1,0:T(8,128)(2,1)}, u32[]{:S(2)}) copy-start(bf16[1024,1024]{1,0:T(8,128)(2,1)} %param.17) | copy-start | bytes 6291460
  7.2 104.9 %all-gather.3.cloned.1.call-start = ((), (), s32[]{:S(2)}) async-start(), calls=%async_computation.4 | async-start | bytes 2113536 | tf_op jit(solution)/shard_map/all_gather | solution.py:43
  11.3 12.3 %copy-start.6 = (s32[1,128]{1,0:T(1,128)S(1)}, s32[1,128]{1,0:T(1,128)}, u32[]{:S(2)}) copy-start(s32[1,128]{1,0:T(1,128)} %param.14) | copy-start | bytes 1540
  27.6 11.8 %copy-start.5 = (s32[512]{0:T(512)S(1)}, s32[512]{0:T(512)}, u32[]{:S(2)}) copy-start(s32[512]{0:T(512)} %param.12) | copy-start | bytes 6148
  27.6 12.2 %copy-start.4 = (s32[512,16]{0,1:T(8,128)S(1)}, s32[512,16]{0,1:T(8,128)}, u32[]{:S(2)}) copy-start(s32[512,16]{0,1:T(8,128)} %param.11) | copy-start | bytes 98308
  27.6 14.2 %copy-start.1 = (bf16[512,1024]{1,0:T(8,128)(2,1)S(1)}, bf16[512,1024]{1,0:T(8,128)(2,1)}, u32[]{:S(2)}) copy-start(bf16[512,1024]{1,0:T(8,128)(2,1)} %param.10) | copy-start | bytes 3145732
  27.6 84.5 %all-to-all-start = ((bf16[128,16,1024]{2,1,0:T(8,128)(2,1)}), bf16[128,16,1024]{2,1,0:T(8,128)(2,1)}, u32[]{:S(2)}, u32[]{:S(2)}) async-start(bf16[128,16,1024]{2,1,0:T(8,128)(2,1)} %broadcast_select_fusion), calls=%async_computation | async-start | bytes 8388608 | tf_op jit(solution)/shard_map/all_to_all | solution.py:41
  39.3 325.4 %all-reduce.5.cloned.1.call-start = ((), (), s32[]{:S(2)}) async-start(), calls=%async_computation.5 | async-start | bytes 16777216 | tf_op jit(solution)/shard_map/psum | solution.py:26
  163.0 8.7 copy-start.7
  163.0 8.7 copy-start.8
  163.0 8.7 copy-start.9
  174.7 3.3 copy-start.2
  181.7 1.2 copy-start.3
  181.7 783.0 %reduce-scatter.2.cloned.1.call-start = ((), (), s32[]{:S(2)}) async-start(), calls=%async_computation.3 | async-start | bytes 4227072 | tf_op jit(solution)/shard_map/reduce_scatter | solution.py:95
  284.1 59.0 %all-to-all-start.1 = ((bf16[128,16,1024]{2,1,0:T(8,128)(2,1)}), bf16[128,16,1024]{2,1,0:T(8,128)(2,1)}, u32[]{:S(2)}, u32[]{:S(2)}) async-start(bf16[128,16,1024]{2,1,0:T(8,128)(2,1)} %bitcast.39), calls=%async_computation.1 | async-start | bytes 8388608 | tf_op jit(solution)/shard_map/all_to_all | solution.py:92
Sparse Core Ops, SparseCore 0:
  11.5 100.4 all-gather.2
  181.9 101.2 all-reduce.4
  285.5 679.1 reduce-scatter.1
